TPU v7x, 128 devices: a whole 4x4x4 slice. The times are simulated.
128 devices in a mesh: row: 8 (over z_hi, y), col: 16 (over x, z_lo, core).
Axes of the slice: x: 4, y: 4, z: 4 (z_hi: 2, z_lo: 2; z = z_hi * 2 + z_lo), core: 2. Of those that a mesh axis runs over, the one named last changes fastest.
Arguments:
- features: bfloat16 [16, 8192, 128], P('col', 'row'), may hold values from 0.099609375 to 3
- relu_mask: int32 [16, 8192, 128], P('col', 'row'), may hold values 0 or 1
- tiles: bfloat16 [8, 16, 184, 256, 256], P('row', 'col'), may hold values from -0.25 to 0.25
- tile_rows: int32 [8, 16, 184], P('row', 'col'), may hold values from 0 to 63, as said below
- tile_cols: int32 [8, 16, 184], P('row', 'col'), may hold values from 0 to 31
- tile_count: int32 [8, 16], P('row', 'col'), may hold values from 23 to 184, as said below
- weight: bfloat16 [128, 128], replicated, may hold values from -0.5 to 0.5
- cotangent: bfloat16 [8, 16384, 128], P('row', 'col'), may hold values from -6 to 6
Outputs:
- out_pre: bfloat16 [8, 16384, 128], P('row', 'col')
- weight_grad: float32 [128, 128], replicated
- input_grad: bfloat16 [16, 8192, 128], P('col', 'row')
Inputs may be any that keep to these rules, and one draw needn't show every extreme that they name: `tile_rows`: within one panel pair the live and dead slots name distinct (block row, block column) pairs. `tile_count`: counts differ widely between panel pairs.
All inputs are finite; a program needn't handle non-finite values. No bound on the sum of `relu_mask` on one device may be relied on, other than what follows from the above.
Results may differ from a plain program's by a relative error of at most 0.022.
Values may be sent and summed in bfloat16 or wider, within the bound.
A program may use at most 192 MiB of HBM per device.

v0:
```python
import jax
import jax.numpy as jnp
from jax import lax
from jax.sharding import PartitionSpec as P


def slot_products(tile_vals, row_ids, col_ids, source, backward):
    tile_size = tile_vals.shape[1]
    feature_width = source.shape[1]
    if backward:
        blocks = source.reshape(-1, tile_size, feature_width)[row_ids]
        products = jnp.einsum("sij,sif->sjf", tile_vals, blocks, preferred_element_type=jnp.float32)
        target_ids = col_ids
    else:
        blocks = source.reshape(-1, tile_size, feature_width)[col_ids]
        products = jnp.einsum("sij,sjf->sif", tile_vals, blocks, preferred_element_type=jnp.float32)
        target_ids = row_ids
    return (products, target_ids)


def apply_tiles(tile_vals, row_ids, col_ids, live_count, source, backward, segments):
    feature_width = source.shape[1]
    slots = tile_vals.shape[0]
    products, target_ids = slot_products(tile_vals, row_ids, col_ids, source, backward)
    live_slots = jnp.arange(slots, dtype=jnp.int32) < live_count
    targets = jnp.arange(segments, dtype=jnp.int32)[:, None] == target_ids[None, :]
    selector = jnp.where(targets & live_slots[None, :], 1.0, 0.0).astype(jnp.float32)
    total = jnp.einsum(
        "rs,sif->rif",
        selector,
        products,
        precision=lax.Precision.HIGHEST,
        preferred_element_type=jnp.float32,
    )
    return total.reshape(-1, feature_width)


def body(features, relu_mask, tiles, tile_rows, tile_cols, tile_count, weight, cotangent):
    tile_size = tiles.shape[3]
    mask_rows = relu_mask[0]
    hidden = features[0] * mask_rows.astype(jnp.bfloat16)
    tile_vals = tiles[0, 0]
    row_ids = tile_rows[0, 0]
    col_ids = tile_cols[0, 0]
    live_count = tile_count[0, 0]
    own_rows = hidden.shape[0]
    row_blocks = own_rows * lax.axis_size("col") // tile_size
    col_blocks = own_rows * lax.axis_size("row") // tile_size
    feat_panel = lax.all_gather(hidden, "row", axis=0, tiled=True)
    forward_terms = apply_tiles(
        tile_vals, row_ids, col_ids, live_count, feat_panel, False, row_blocks
    )
    forward_terms = lax.optimization_barrier(forward_terms.astype(jnp.bfloat16)).astype(jnp.float32)
    aggregate = lax.psum_scatter(
        forward_terms.astype(jnp.bfloat16), "col", scatter_dimension=0, tiled=True
    )
    out_pre = jnp.dot(aggregate, weight, preferred_element_type=jnp.float32).astype(jnp.bfloat16)
    cot_rows = cotangent[0]
    weight_term = lax.dot_general(
        aggregate, cot_rows, (((0,), (0,)), ((), ())), preferred_element_type=jnp.float32
    )
    grad_scale = 1.0 / jnp.sqrt(jnp.float32(own_rows * lax.axis_size("row") * lax.axis_size("col")))
    weight_grad = lax.psum(weight_term, ("row", "col")) * grad_scale
    grad_rows = lax.dot_general(
        cot_rows, weight, (((1,), (1,)), ((), ())), preferred_element_type=jnp.float32
    )
    grad_rows = lax.all_gather(grad_rows.astype(jnp.bfloat16), "col", axis=0, tiled=True)
    back_terms = apply_tiles(tile_vals, row_ids, col_ids, live_count, grad_rows, True, col_blocks)
    back_terms = lax.optimization_barrier(back_terms.astype(jnp.bfloat16)).astype(jnp.float32)
    summed = lax.psum_scatter(
        back_terms.astype(jnp.bfloat16), "row", scatter_dimension=0, tiled=True
    ).astype(jnp.float32)
    input_grad = (summed * mask_rows.astype(jnp.float32)).astype(jnp.bfloat16)
    return (out_pre[None], weight_grad, input_grad[None])


def solution(mesh):
    placed = (
        P("col", "row", None),
        P("col", "row", None),
        P("row", "col", None, None, None),
        P("row", "col", None),
        P("row", "col", None),
        P("row", "col"),
        P(),
        P("row", "col", None),
    )
    return jax.shard_map(
        body,
        mesh=mesh,
        in_specs=placed,
        out_specs=(P("row", "col", None), P(), P("col", "row", None)),
        check_vma=False,
    )
```

profile of v0, /device:TPU:1, one launch (start us, length us, event | category | flops | bytes accessed | tf_op | source)
XLA Modules:
  0.0 451.2 jit_solution(6644754055595961643)
XLA Ops:
  7.2 0.0 copy-start
  7.2 0.0 all-gather.6.cloned.1.call-start
  7.2 1.9 convert_multiply_fusion
  9.1 0.0 all-gather.6.cloned.1.call-update
  9.1 0.0 all-gather.4.cloned.1.call-start
  9.2 0.0 copy-done
  9.2 1.7 convolution_convert_fusion
  10.9 0.0 all-gather.4.cloned.1.call-update
  10.9 0.0 reduce-scatter.3.cloned.1.call-start
  11.6 0.7 compare_select_fusion.1
  12.3 55.5 %all-gather.6.cloned.1.call-done = bf16[1,8192,128]{2,1,0:T(8,128)(2,1)} async-done(((bf16[1,1024,128]{2,1,0:T(8,128)(2,1)}), bf16[1,8192,128]{2,1,0:T(8,128)(2,1)}) %all-gather.6.cloned.1.call-update) | async-done | bytes 2097168 | tf_op jit(solution)/shard_map/all_gather | solution.py:49
  67.9 9.7 %gather_fusion = bf16[184,256,128]{2,1,0:T(8,128)(2,1)} fusion(bf16[32,256,128]{2,1,0:T(8,128)(2,1)} %bitcast.56, s32[1024]{0:T(1024)S(1)} %pad_clamp_fusion.1), kind=kCustom, calls=%fused_computation | custom fusion | bytes 24117984 | tf_op jit(solution)/shard_map/gather | solution.py:15
  77.5 21.6 %fusion.6 = f32[184,128,256]{2,1,0:T(8,128)} fusion(bf16[184,256,128]{2,1,0:T(8,128)(2,1)} %gather_fusion, bf16[1,1,184,256,256]{4,3,2,1,0:T(8,128)(2,1)} %param.10), kind=kOutput, calls=%fused_computation.8 | convolution fusion | flops 3087007744 | bytes 60293120 | tf_op jit(solution)/shard_map/sij,sjf->sif/dot_general | solution.py:16
  99.1 0.0 copy-start.3
  99.1 24.6 %copy.13 = f32[184,128,256]{1,0,2:T(8,128)} copy(f32[184,128,256]{2,1,0:T(8,128)} %fusion.6) | data formatting | bytes 48234496 | tf_op jit(solution)/shard_map/sij,sjf->sif/dot_general | solution.py:16
  123.7 0.0 copy-done.3
  123.7 20.8 %fusion.8 = bf16[64,256,128]{2,0,1:T(8,128)(2,1)S(1)} fusion(f32[184,128,256]{1,0,2:T(8,128)} %copy.13, s32[184]{0:T(256)S(1)} %bitcast.60, pred[184]{0:T(512)(128)(4,1)S(1)} %iota_compare_fusion.2), kind=kOutput, calls=%fused_computation.10 | convolution fusion | flops 4632644096 | bytes 28312472 | tf_op jit(solution)/shard_map/rs,sif->rif/dot_general | solution.py:28
  144.5 4.7 %copy.11 = bf16[64,256,128]{2,1,0:T(8,128)(2,1)} copy(bf16[64,256,128]{2,0,1:T(8,128)(2,1)S(1)} %fusion.8) | data formatting | bytes 8388608 | tf_op jit(solution)/shard_map/convert_element_type | solution.py:53
  149.1 0.0 reduce-scatter.3.cloned.1.call-update
  149.2 0.0 reduce-scatter.5.cloned.1.call-start
  149.2 0.0 all-gather.4.cloned.1.call-done
  149.3 10.3 %gather_fusion.1 = bf16[184,256,128]{2,1,0:T(8,128)(2,1)} fusion(bf16[64,256,128]{2,1,0:T(8,128)(2,1)} %bitcast.57, s32[1024]{0:T(1024)S(1)} %pad_clamp_fusion), kind=kCustom, calls=%fused_computation.1 | custom fusion | bytes 24117984 | tf_op jit(solution)/shard_map/gather | solution.py:11
  159.5 22.0 %fusion.4 = f32[184,128,256]{2,1,0:T(8,128)} fusion(bf16[184,256,128]{2,1,0:T(8,128)(2,1)} %gather_fusion.1, bf16[1,1,184,256,256]{4,3,2,1,0:T(8,128)(2,1)} %param.10), kind=kOutput, calls=%fused_computation.6 | convolution fusion | flops 3087007744 | bytes 60293120 | tf_op jit(solution)/shard_map/sij,sif->sjf/dot_general | solution.py:12
  181.6 0.0 copy-start.4
  181.6 24.6 %copy.14 = f32[184,128,256]{1,0,2:T(8,128)} copy(f32[184,128,256]{2,1,0:T(8,128)} %fusion.4) | data formatting | bytes 48234496 | tf_op jit(solution)/shard_map/sij,sif->sjf/dot_general | solution.py:12
  206.2 0.0 copy-done.4
  206.2 0.0 copy-start.2
  206.2 0.0 copy-start.1
  206.2 17.1 %fusion.11 = bf16[32,256,128]{2,0,1:T(8,128)(2,1)S(1)} fusion(f32[184,128,256]{1,0,2:T(8,128)} %copy.14, s32[184]{0:T(256)S(1)} %bitcast.61, pred[184]{0:T(512)(128)(4,1)S(1)} %iota_compare_fusion.2), kind=kOutput, calls=%fused_computation.11 | convolution fusion | flops 2316322048 | bytes 26215320 | tf_op jit(solution)/shard_map/rs,sif->rif/dot_general | solution.py:28
  223.3 2.1 copy.12
  225.4 0.0 reduce-scatter.5.cloned.1.call-update
  225.4 0.0 all-reduce.2.cloned.1.call-start
  225.5 0.0 reduce-scatter.3.cloned.1.call-done
  225.5 1.9 fusion.18
  227.4 0.0 all-reduce.2.cloned.1.call-update
  227.4 0.0 copy-done.2
  227.4 1.9 fusion.14
  229.3 70.3 %reduce-scatter.5.cloned.1.call-done = bf16[1024,128]{1,0:T(8,128)(2,1)} async-done(((bf16[8192,128]{1,0:T(8,128)(2,1)}), bf16[1024,128]{1,0:T(8,128)(2,1)}) %reduce-scatter.5.cloned.1.call-update) | async-done | bytes 262160 | tf_op jit(solution)/shard_map/reduce_scatter | solution.py:70
  299.6 0.0 copy-done.1
  299.6 1.7 fusion.16
  301.3 141.9 %all-reduce.2.cloned.1.call-done = f32[128,128]{1,0:T(8,128)} async-done(((f32[128,128]{1,0:T(8,128)}), f32[128,128]{1,0:T(8,128)}) %all-reduce.2.cloned.1.call-update) | async-done | bytes 65552 | tf_op jit(solution)/shard_map/psum | solution.py:63
  443.2 1.5 broadcast_multiply_fusion
  (4 shorter events, 0.0 us)
Async XLA Ops:
  7.2 2.0 copy-start
  7.2 60.7 %all-gather.6.cloned.1.call-start = ((), (), s32[]{:S(2)}) async-start(), calls=%async_computation.6 | async-start | bytes 2359296 | tf_op jit(solution)/shard_map/all_gather | solution.py:49
  9.1 140.1 %all-gather.4.cloned.1.call-start = ((), (), s32[]{:S(2)}) async-start(), calls=%async_computation.4 | async-start | bytes 4456448 | tf_op jit(solution)/shard_map/all_gather | solution.py:67
  10.9 214.6 %reduce-scatter.3.cloned.1.call-start = ((), (), s32[]{:S(2)}) async-start(), calls=%async_computation.2 | async-start | bytes 4456448 | tf_op jit(solution)/shard_map/reduce_scatter | solution.py:54
  99.1 24.6 %copy-start.3 = (s32[1,1,184]{2,1,0:T(1,128)S(1)}, s32[1,1,184]{2,1,0:T(1,128)}, u32[]{:S(2)}) copy-start(s32[1,1,184]{2,1,0:T(1,128)} %param.11) | copy-start | bytes 2212
  149.2 150.4 %reduce-scatter.5.cloned.1.call-start = ((), (), s32[]{:S(2)}) async-start(), calls=%async_computation.5 | async-start | bytes 2359296 | tf_op jit(solution)/shard_map/reduce_scatter | solution.py:70
  181.6 24.6 %copy-start.4 = (s32[1,1,184]{2,1,0:T(1,128)S(1)}, s32[1,1,184]{2,1,0:T(1,128)}, u32[]{:S(2)}) copy-start(s32[1,1,184]{2,1,0:T(1,128)} %param.12) | copy-start | bytes 2212
  206.2 21.2 %copy-start.2 = (bf16[128,128]{1,0:T(8,128)(2,1)S(1)}, bf16[128,128]{1,0:T(8,128)(2,1)}, u32[]{:S(2)}) copy-start(bf16[128,128]{1,0:T(8,128)(2,1)} %param.14) | copy-start | bytes 98308
  206.2 93.4 %copy-start.1 = (s32[1,1024,128]{2,1,0:T(8,128)S(1)}, s32[1,1024,128]{2,1,0:T(8,128)}, u32[]{:S(2)}) copy-start(s32[1,1024,128]{2,1,0:T(8,128)} %param.9) | copy-start | bytes 1572868
  225.4 217.8 %all-reduce.2.cloned.1.call-start = ((), (), s32[]{:S(2)}) async-start(), calls=%async_computation.3 | async-start | bytes 131072 | tf_op jit(solution)/shard_map/psum | solution.py:63
Sparse Core Ops, SparseCore 0:
  10.9 56.9 all-gather.5
  70.1 37.8 all-gather.3
  149.3 63.9 reduce-scatter.2
  225.6 74.0 reduce-scatter.4
  305.5 137.6 all-reduce.1
where the time goes:
time: 452 us; the launch traced here: 451 us
  waiting for transfers between devices  268 us (59%)
  matrix products  86.9 us (19%)
  local copies, waits for them, and re-layouts  75.9 us (17%)
  between operations  14.5 us (3%)
  other arithmetic  5.8 us (1%)
    psum x1, waiting for transfers between devices, body(): weight_grad = lax.psum(weight_term, ('row', 'col')) * grad_scale  142 us
    reduce_scatter x1, waiting for transfers between devices, body(): lax.psum_scatter(back_terms.astype(jnp.bfloat16), 'row', scatter_dimensio...  70.3 us
    all_gather x1, waiting for transfers between devices, body(): feat_panel = lax.all_gather(hidden, 'row', axis=0, tiled=True)  55.5 us
    dot_general x2, matrix products, apply_tiles(): jnp.einsum('rs,sif->rif', selector, products, precision=lax.Precision.HIG...  37.8 us
    dot_general x1, local copies, waits for them, and re-layouts, slot_products(): jnp.einsum('sij,sif->sjf', tile_vals, blocks, preferred_element_type=jnp....  24.6 us
    dot_general x1, local copies, waits for them, and re-layouts, slot_products(): jnp.einsum('sij,sjf->sif', tile_vals, blocks, preferred_element_type=jnp....  24.6 us
    dot_general x1, matrix products, slot_products(): jnp.einsum('sij,sif->sjf', tile_vals, blocks, preferred_element_type=jnp....  22 us
    dot_general x1, matrix products, slot_products(): jnp.einsum('sij,sjf->sif', tile_vals, blocks, preferred_element_type=jnp....  21.6 us
  transfers between devices with their start and end apart: 5, of which 3 were waited for; matrix products, arithmetic and copies ran while one was open for 37% of the time, Pallas kernels for 0%

commit v1 on v0

--- a/solution.py
+++ b/solution.py
@@ -46,7 +46,9 @@
     own_rows = hidden.shape[0]
     row_blocks = own_rows * lax.axis_size("col") // tile_size
     col_blocks = own_rows * lax.axis_size("row") // tile_size
-    feat_panel = lax.all_gather(hidden, "row", axis=0, tiled=True)
+    feat_panel = jnp.concatenate(
+        lax.all_to_all(jnp.stack([hidden] * lax.axis_size("row")), "row", 0, 0), axis=0
+    )
     forward_terms = apply_tiles(
         tile_vals, row_ids, col_ids, live_count, feat_panel, False, row_blocks
     )

time: 452 us -> 426 us (0.942)
  waiting for transfers between devices: 268 us -> 233 us
  starting transfers between devices: 0.21 us -> 8.49 us
    all_gather x1 -> x0, waiting for transfers between devices: 55.5 us -> none  [body(): feat_panel = lax.all_gather(hidden, 'row', axis=0, tiled=True)]
    all_to_all x0 -> x1, waiting for transfers between devices: none -> 27.2 us  [body(): lax.all_to_all(jnp.stack([hidden] * lax.axis_size('row')), 'row', 0, 0)]
    psum x1, waiting for transfers between devices: 142 us -> 123 us  [body(): weight_grad = lax.psum(weight_term, ('row', 'col')) * grad_scale]
    reduce_scatter x1, waiting for transfers between devices: 0.02 us -> 9.41 us  [body(): lax.psum_scatter(forward_terms.astype(jnp.bfloat16), 'col', scatter_dimen...]
    all_to_all x0 -> x1, starting transfers between devices: none -> 8.33 us  [body(): lax.all_to_all(jnp.stack([hidden] * lax.axis_size('row')), 'row', 0, 0)]
  transfers between devices with their start and end apart: 5 -> 5, of which waited for: 3 -> 4; matrix products, arithmetic and copies ran while one was open for 37% -> 38% of each run, Pallas kernels for 0% -> 0%
where the time goes in v1:
time: 426 us; the launch traced here: 424 us
  waiting for transfers between devices  233 us (55%)
  matrix products  85.9 us (20%)
  local copies, waits for them, and re-layouts  76.7 us (18%)
  between operations  14.5 us (3%)
  starting transfers between devices  8.49 us (2%)
  other arithmetic  5.07 us (1%)
    psum x1, waiting for transfers between devices, body(): weight_grad = lax.psum(weight_term, ('row', 'col')) * grad_scale  123 us
    reduce_scatter x1, waiting for transfers between devices, body(): lax.psum_scatter(back_terms.astype(jnp.bfloat16), 'row', scatter_dimensio...  73.6 us
    dot_general x2, matrix products, apply_tiles(): jnp.einsum('rs,sif->rif', selector, products, precision=lax.Precision.HIG...  37.9 us
    all_to_all x1, waiting for transfers between devices, body(): lax.all_to_all(jnp.stack([hidden] * lax.axis_size('row')), 'row', 0, 0)  27.2 us
    dot_general x1, local copies, waits for them, and re-layouts, slot_products(): jnp.einsum('sij,sif->sjf', tile_vals, blocks, preferred_element_type=jnp....  24.5 us
    dot_general x1, local copies, waits for them, and re-layouts, slot_products(): jnp.einsum('sij,sjf->sif', tile_vals, blocks, preferred_element_type=jnp....  24.5 us
    dot_general x1, matrix products, slot_products(): jnp.einsum('sij,sif->sjf', tile_vals, blocks, preferred_element_type=jnp....  22.3 us
    dot_general x1, matrix products, slot_products(): jnp.einsum('sij,sjf->sif', tile_vals, blocks, preferred_element_type=jnp....  21.2 us
  transfers between devices with their start and end apart: 5, of which 4 were waited for; matrix products, arithmetic and copies ran while one was open for 38% of the time, Pallas kernels for 0%

profile of v1, /device:TPU:1, one launch (start us, length us, event | category | flops | bytes accessed | tf_op | source)
XLA Modules:
  0.0 424.1 jit_solution(17459217903747370980)
XLA Ops:
  7.2 0.0 copy-start
  7.2 0.0 all-gather.2.cloned.1.call-start
  7.2 0.9 copy-done
  8.1 1.7 convolution_convert_fusion
  9.8 0.0 all-gather.2.cloned.1.call-update
  9.8 1.2 multiply_bitcast_fusion
  11.0 1.6 stack.5
  12.6 8.3 %all-to-all-start = ((bf16[8,1024,128]{2,1,0:T(8,128)(2,1)}), bf16[8,1024,128]{2,1,0:T(8,128)(2,1)S(1)}, u32[]{:S(2)}, u32[]{:S(2)}) async-start(bf16[8,1024,128]{2,1,0:T(8,128)(2,1)} %stack.5), calls=%async_computation | async-start | bytes 4194304 | tf_op jit(solution)/shard_map/all_to_all | solution.py:50
  20.9 0.0 reduce-scatter.3.cloned.1.call-start
  21.6 0.7 compare_select_fusion.1
  22.3 27.2 %all-to-all-done = bf16[8,1024,128]{2,1,0:T(8,128)(2,1)S(1)} async-done(((bf16[8,1024,128]{2,1,0:T(8,128)(2,1)}), bf16[8,1024,128]{2,1,0:T(8,128)(2,1)S(1)}, u32[]{:S(2)}, u32[]{:S(2)}) %all-to-all-start) | async-done | bytes 2097184 | tf_op jit(solution)/shard_map/all_to_all | solution.py:50
  49.5 8.1 %gather_fusion = bf16[184,256,128]{2,1,0:T(8,128)(2,1)} fusion(bf16[32,256,128]{2,1,0:T(8,128)(2,1)S(1)} %bitcast.58, s32[1024]{0:T(1024)S(1)} %pad_clamp_fusion.1), kind=kCustom, calls=%fused_computation | custom fusion | bytes 24117984 | tf_op jit(solution)/shard_map/gather | solution.py:15
  57.6 21.2 %fusion.6 = f32[184,128,256]{2,1,0:T(8,128)} fusion(bf16[184,256,128]{2,1,0:T(8,128)(2,1)} %gather_fusion, bf16[1,1,184,256,256]{4,3,2,1,0:T(8,128)(2,1)} %param.10), kind=kOutput, calls=%fused_computation.8 | convolution fusion | flops 3087007744 | bytes 60293120 | tf_op jit(solution)/shard_map/sij,sjf->sif/dot_general | solution.py:16
  78.8 0.0 copy-start.4
  78.8 24.5 %copy.13 = f32[184,128,256]{1,0,2:T(8,128)} copy(f32[184,128,256]{2,1,0:T(8,128)} %fusion.6) | data formatting | bytes 48234496 | tf_op jit(solution)/shard_map/sij,sjf->sif/dot_general | solution.py:16
  103.4 0.0 copy-done.4
  103.4 20.8 %fusion.8 = bf16[64,256,128]{2,0,1:T(8,128)(2,1)S(1)} fusion(f32[184,128,256]{1,0,2:T(8,128)} %copy.13, s32[184]{0:T(256)S(1)} %bitcast.62, pred[184]{0:T(512)(128)(4,1)S(1)} %iota_compare_fusion.2), kind=kOutput, calls=%fused_computation.10 | convolution fusion | flops 4632644096 | bytes 28312472 | tf_op jit(solution)/shard_map/rs,sif->rif/dot_general | solution.py:28
  124.2 4.7 %copy.11 = bf16[64,256,128]{2,1,0:T(8,128)(2,1)} copy(bf16[64,256,128]{2,0,1:T(8,128)(2,1)S(1)} %fusion.8) | data formatting | bytes 8388608 | tf_op jit(solution)/shard_map/convert_element_type | solution.py:55
  128.8 0.0 reduce-scatter.3.cloned.1.call-update
  128.8 0.0 all-reduce.2.cloned.1.call-start
  128.9 0.0 all-gather.2.cloned.1.call-done
  128.9 10.3 %gather_fusion.1 = bf16[184,256,128]{2,1,0:T(8,128)(2,1)} fusion(bf16[64,256,128]{2,1,0:T(8,128)(2,1)} %bitcast.59, s32[1024]{0:T(1024)S(1)} %pad_clamp_fusion), kind=kCustom, calls=%fused_computation.1 | custom fusion | bytes 24117984 | tf_op jit(solution)/shard_map/gather | solution.py:11
  139.2 22.3 %fusion.4 = f32[184,128,256]{2,1,0:T(8,128)} fusion(bf16[184,256,128]{2,1,0:T(8,128)(2,1)} %gather_fusion.1, bf16[1,1,184,256,256]{4,3,2,1,0:T(8,128)(2,1)} %param.10), kind=kOutput, calls=%fused_computation.6 | convolution fusion | flops 3087007744 | bytes 60293120 | tf_op jit(solution)/shard_map/sij,sif->sjf/dot_general | solution.py:12
  161.5 0.0 copy-start.5
  161.5 24.5 %copy.14 = f32[184,128,256]{1,0,2:T(8,128)} copy(f32[184,128,256]{2,1,0:T(8,128)} %fusion.4) | data formatting | bytes 48234496 | tf_op jit(solution)/shard_map/sij,sif->sjf/dot_general | solution.py:12
  186.0 9.4 %reduce-scatter.3.cloned.1.call-done = bf16[1024,128]{1,0:T(8,128)(2,1)} async-done(((bf16[16384,128]{1,0:T(8,128)(2,1)}), bf16[1024,128]{1,0:T(8,128)(2,1)}) %reduce-scatter.3.cloned.1.call-update) | async-done | bytes 262160 | tf_op jit(solution)/shard_map/reduce_scatter | solution.py:56
  195.5 1.8 fusion.18
  197.3 0.0 all-reduce.2.cloned.1.call-update
  197.3 0.0 reduce-scatter.5.cloned.1.call-start
  197.4 0.0 copy-done.5
  197.4 0.0 copy-start.2
  197.4 0.0 copy-start.3
  197.4 0.0 copy-start.1
  197.4 17.1 %fusion.11 = bf16[32,256,128]{2,0,1:T(8,128)(2,1)S(1)} fusion(f32[184,128,256]{1,0,2:T(8,128)} %copy.14, s32[184]{0:T(256)S(1)} %bitcast.63, pred[184]{0:T(512)(128)(4,1)S(1)} %iota_compare_fusion.2), kind=kOutput, calls=%fused_computation.11 | convolution fusion | flops 2316322048 | bytes 26215320 | tf_op jit(solution)/shard_map/rs,sif->rif/dot_general | solution.py:28
  214.5 2.1 copy.12
  216.6 0.0 reduce-scatter.5.cloned.1.call-update
  216.7 0.0 copy-done.2
  216.7 0.0 copy-done.3
  216.7 0.9 fusion.14
  217.6 123.2 %all-reduce.2.cloned.1.call-done = f32[128,128]{1,0:T(8,128)} async-done(((f32[128,128]{1,0:T(8,128)}), f32[128,128]{1,0:T(8,128)}) %all-reduce.2.cloned.1.call-update) | async-done | bytes 65552 | tf_op jit(solution)/shard_map/psum | solution.py:65
  340.8 1.5 broadcast_multiply_fusion
  342.2 73.6 %reduce-scatter.5.cloned.1.call-done = bf16[1024,128]{1,0:T(8,128)(2,1)} async-done(((bf16[8192,128]{1,0:T(8,128)(2,1)}), bf16[1024,128]{1,0:T(8,128)(2,1)}) %reduce-scatter.5.cloned.1.call-update) | async-done | bytes 262160 | tf_op jit(solution)/shard_map/reduce_scatter | solution.py:72
  415.8 0.0 copy-done.1
  415.8 1.7 fusion.16
  (4 shorter events, 0.0 us)
Async XLA Ops:
  7.2 1.0 copy-start
  7.2 121.8 %all-gather.2.cloned.1.call-start = ((), (), s32[]{:S(2)}) async-start(), calls=%async_computation.5 | async-start | bytes 4456448 | tf_op jit(solution)/shard_map/all_gather | solution.py:69
  12.6 36.9 %all-to-all-start = ((bf16[8,1024,128]{2,1,0:T(8,128)(2,1)}), bf16[8,1024,128]{2,1,0:T(8,128)(2,1)S(1)}, u32[]{:S(2)}, u32[]{:S(2)}) async-start(bf16[8,1024,128]{2,1,0:T(8,128)(2,1)} %stack.5), calls=%async_computation | async-start | bytes 4194304 | tf_op jit(solution)/shard_map/all_to_all | solution.py:50
  20.9 174.5 %reduce-scatter.3.cloned.1.call-start = ((), (), s32[]{:S(2)}) async-start(), calls=%async_computation.3 | async-start | bytes 4456448 | tf_op jit(solution)/shard_map/reduce_scatter | solution.py:56
  78.8 24.5 %copy-start.4 = (s32[1,1,184]{2,1,0:T(1,128)S(1)}, s32[1,1,184]{2,1,0:T(1,128)}, u32[]{:S(2)}) copy-start(s32[1,1,184]{2,1,0:T(1,128)} %param.11) | copy-start | bytes 2212
  128.8 211.9 %all-reduce.2.cloned.1.call-start = ((), (), s32[]{:S(2)}) async-start(), calls=%async_computation.4 | async-start | bytes 131072 | tf_op jit(solution)/shard_map/psum | solution.py:65
  161.5 35.9 %copy-start.5 = (s32[1,1,184]{2,1,0:T(1,128)S(1)}, s32[1,1,184]{2,1,0:T(1,128)}, u32[]{:S(2)}) copy-start(s32[1,1,184]{2,1,0:T(1,128)} %param.12) | copy-start | bytes 2212
  197.3 218.5 %reduce-scatter.5.cloned.1.call-start = ((), (), s32[]{:S(2)}) async-start(), calls=%async_computation.6 | async-start | bytes 2359296 | tf_op jit(solution)/shard_map/reduce_scatter | solution.py:72
  197.4 19.3 %copy-start.2 = (bf16[1024,128]{1,0:T(8,128)(2,1)S(1)}, bf16[1024,128]{1,0:T(8,128)(2,1)}, u32[]{:S(2)}) copy-start(bf16[1024,128]{1,0:T(8,128)(2,1)} %reduce-scatter.3.cloned.1.call-done) | copy-start | bytes 786436
  197.4 19.3 %copy-start.3 = (bf16[128,128]{1,0:T(8,128)(2,1)S(1)}, bf16[128,128]{1,0:T(8,128)(2,1)}, u32[]{:S(2)}) copy-start(bf16[128,128]{1,0:T(8,128)(2,1)} %param.14) | copy-start | bytes 98308
  197.4 218.4 %copy-start.1 = (s32[1,1024,128]{2,1,0:T(8,128)S(1)}, s32[1,1024,128]{2,1,0:T(8,128)}, u32[]{:S(2)}) copy-start(s32[1,1024,128]{2,1,0:T(8,128)} %param.9) | copy-start | bytes 1572868
Sparse Core Ops, SparseCore 0:
  10.3 60.7 all-gather.1
  129.0 66.4 reduce-scatter.2
  200.8 139.9 all-reduce.1
  344.8 70.9 reduce-scatter.4
